TPU v7x, 32 devices: a whole 2x2x4 slice. The times are simulated.
32 devices in a mesh: dp: 8 (over z, x), seq: 4 (over y, core).
Axes of the slice: x: 2, y: 2, z: 4, core: 2. Of those that a mesh axis runs over, the one named last changes fastest.
Arguments:
- spatial_qkv: bfloat16 [8, 3, 4, 128, 1152], P('dp', None, 'seq'), may hold values from -24 to 24
- temporal_qkv: bfloat16 [8, 3, 4, 128, 1152], P('dp', None, 'seq'), may hold values from -24 to 24
- cotangent: bfloat16 [8, 4, 128, 1152], P('dp', 'seq'), may hold values from -6 to 6
- spatial_gate: float32 [8, 1152], P('dp'), may hold values from -4 to 4
- temporal_gate: float32 [8, 1152], P('dp'), may hold values from -4 to 4
- temporal_proj: bfloat16 [1152, 1152], replicated, may hold values from -0.1875 to 0.1875
- live_counts: int32 [8, 2], P('dp'), may hold values from 2 to 128, as said below
Outputs:
- temporal_qkv_grad: bfloat16 [8, 3, 4, 128, 1152], P('dp', None, 'seq')
- spatial_proj_grad: float32 [1152, 1152], P('seq', 'dp')
- temporal_proj_grad: float32 [1152, 1152], P('seq', 'dp')
Inputs may be any that keep to these rules, and one draw needn't show every extreme that they name: live_counts[g, 0] counts a clip's live frames, at most 4; live_counts[g, 1] counts the live positions of each of its frames, at most 128; in every draw some clip has all 4 frames and all 128 positions live.
All inputs are finite; a program needn't handle non-finite values.
Results may differ from a plain program's by a relative error of at most 0.015.
Values may be sent and summed in bfloat16 or wider, within the bound.
A program may use at most 64 MiB of HBM per device.

v0:
```python
import jax
import jax.numpy as jnp
from jax import lax
from jax.sharding import PartitionSpec as P

HEADS = 16
HD = 72


def attend(queries, key_block, value_block, key_keep, score_form, mix_form):
    head_split = queries.shape[:-1] + (HEADS, HD)
    q_heads = queries.reshape(head_split)
    k_heads = key_block.reshape(head_split)
    v_heads = value_block.reshape(head_split)
    scores = jnp.einsum(score_form, q_heads, k_heads, preferred_element_type=jnp.float32) * HD ** (
        -0.5
    )
    scores = jnp.where(key_keep[:, None, None, :], scores, -1e30)
    shifted = scores - jnp.max(scores, axis=-1, keepdims=True)
    expo = jnp.exp(shifted)
    attention_weights = (expo / jnp.sum(expo, axis=-1, keepdims=True)).astype(jnp.bfloat16)
    mixed = jnp.einsum(mix_form, attention_weights, v_heads, preferred_element_type=jnp.float32)
    return mixed.reshape(queries.shape)


def body(
    spatial_qkv, temporal_qkv, cotangent, spatial_gate, temporal_gate, temporal_proj, live_counts
):
    spatial = spatial_qkv[0]
    temporal = temporal_qkv[0]
    incoming = cotangent[0]
    frame_count, position_count, width = incoming.shape
    group_size = lax.axis_size("seq")
    member = lax.axis_index("seq")
    live_frames = live_counts[0, 0]
    live_positions = live_counts[0, 1]
    frame_ids = member * frame_count + jnp.arange(frame_count, dtype=jnp.int32)
    position_ids = jnp.arange(position_count, dtype=jnp.int32)
    token_mask = (
        (frame_ids[:, None] < live_frames) & (position_ids[None, :] < live_positions)
    ).astype(jnp.float32)
    flowing = token_mask[:, :, None] * incoming.astype(jnp.float32)
    temporal_error = (flowing * temporal_gate[0]).astype(jnp.bfloat16)
    temporal_back = lax.dot_general(
        temporal_error, temporal_proj, (((2,), (1,)), ((), ())), preferred_element_type=jnp.float32
    ).astype(jnp.bfloat16)
    stacked = jnp.concatenate([temporal, temporal_back[None]], axis=0)
    exchanged = lax.all_to_all(stacked, "seq", split_axis=2, concat_axis=1, tiled=True)
    spatial_keep = position_ids[None, :] < live_positions
    spatial_out = attend(
        spatial[0], spatial[1], spatial[2], spatial_keep, "bqhd,bkhd->bhqk", "bhqk,bkhd->bqhd"
    ).astype(jnp.bfloat16)
    total_frames = exchanged.shape[1]
    slice_positions = exchanged.shape[2]
    temporal_keep = jnp.broadcast_to(
        jnp.arange(total_frames, dtype=jnp.int32)[None, :] < live_frames,
        (slice_positions, total_frames),
    )

    def temporal_attend(queries, key_block, value_block):
        return attend(
            queries, key_block, value_block, temporal_keep, "qbhd,kbhd->bhqk", "bhqk,kbhd->qbhd"
        )

    temporal_result, pullback = jax.vjp(temporal_attend, exchanged[0], exchanged[1], exchanged[2])
    temporal_out = temporal_result.astype(jnp.bfloat16)
    input_grads = jnp.stack(pullback(exchanged[3].astype(jnp.float32)))
    temporal_frames = lax.all_to_all(temporal_out, "seq", split_axis=0, concat_axis=1, tiled=True)
    grads_home = lax.all_to_all(input_grads, "seq", split_axis=1, concat_axis=2, tiled=True)
    tokens = frame_count * position_count
    flat_spatial = spatial_out.reshape(tokens, width)
    flat_temporal = temporal_frames.reshape(tokens, width)
    slice_width = width // group_size
    column_spatial, column_temporal = (
        lax.all_to_all(flat_spatial, "seq", split_axis=1, concat_axis=0, tiled=True),
        lax.all_to_all(flat_temporal, "seq", split_axis=1, concat_axis=0, tiled=True),
    )
    spatial_scale = spatial_gate[0]
    temporal_scale = temporal_gate[0]
    starting = jnp.zeros((slice_width, 2, width), jnp.float32)
    cot_piece = lax.all_gather(incoming.reshape(tokens, width), "seq", axis=0, tiled=True)
    shards = cot_piece.shape[0] // tokens

    def one_block(block, total):
        offset = (block * tokens).astype(jnp.int32)
        rows = lax.dynamic_slice_in_dim(cot_piece, offset, tokens, 0)
        token_index = offset + jnp.arange(tokens, dtype=jnp.int32)
        frame_of = token_index // position_count
        position_of = token_index % position_count
        row_keep = ((frame_of < live_frames) & (position_of < live_positions)).astype(jnp.float32)
        masked_rows = row_keep[:, None] * rows.astype(jnp.float32)
        error_first = (masked_rows * spatial_scale).astype(jnp.bfloat16)
        error_second = (masked_rows * temporal_scale).astype(jnp.bfloat16)
        cols_first = lax.dynamic_slice_in_dim(column_spatial, offset, tokens, 0)
        cols_second = lax.dynamic_slice_in_dim(column_temporal, offset, tokens, 0)
        part_first = lax.dot_general(
            cols_first, error_first, (((0,), (0,)), ((), ())), preferred_element_type=jnp.float32
        )
        part_second = lax.dot_general(
            cols_second, error_second, (((0,), (0,)), ((), ())), preferred_element_type=jnp.float32
        )
        part_first = part_first.astype(jnp.bfloat16).astype(jnp.float32)
        part_second = part_second.astype(jnp.bfloat16).astype(jnp.float32)
        return total + jnp.stack([part_first, part_second], axis=1)

    partial_sum = lax.fori_loop(0, shards, one_block, starting)
    summed = lax.psum_scatter(partial_sum, "dp", scatter_dimension=2, tiled=True)
    return (grads_home[None], summed[:, 0], summed[:, 1])


def solution(mesh):
    return jax.shard_map(
        body,
        mesh=mesh,
        in_specs=(
            P("dp", None, "seq", None, None),
            P("dp", None, "seq", None, None),
            P("dp", "seq", None, None),
            P("dp", None),
            P("dp", None),
            P(),
            P("dp", None),
        ),
        out_specs=(P("dp", None, "seq", None, None), P("seq", "dp"), P("seq", "dp")),
        check_vma=False,
    )
```

profile of v0, /device:TPU:1, one launch (start us, length us, event | category | flops | bytes accessed | tf_op | source)
XLA Modules:
  0.0 222.5 jit_solution(1551317566120722395)
XLA Ops:
  14.6 2.2 %pad_maximum_fusion = bf16[4,1,128,1152]{3,0,1,2:T(4,128)(2,1)} fusion(bf16[1,1,128,1152]{3,0,1,2:T(2,128)(2,1)S(1)} %copy.89, bf16[3,1,128,1152]{3,0,1,2:T(4,128)(2,1)S(1)} %bitcast.78), kind=kLoop, calls=%fused_computation.45 | loop fusion | flops 2359296 | bytes 2359296 | tf_op jit(solution)/shard_map/concatenate | solution.py:47
  16.9 4.3 %all-to-all-start = ((bf16[4,1,128,1152]{3,0,1,2:T(4,128)(2,1)}), bf16[4,1,128,1152]{3,0,1,2:T(4,128)(2,1)}, u32[]{:S(2)}, u32[]{:S(2)}) async-start(bf16[4,1,128,1152]{3,0,1,2:T(4,128)(2,1)} %pad_maximum_fusion), calls=%async_computation | async-start | bytes 2359296 | tf_op jit(solution)/shard_map/all_to_all | solution.py:48
  29.2 11.2 %all-to-all-done = bf16[4,1,128,1152]{3,0,1,2:T(4,128)(2,1)} async-done(((bf16[4,1,128,1152]{3,0,1,2:T(4,128)(2,1)}), bf16[4,1,128,1152]{3,0,1,2:T(4,128)(2,1)}, u32[]{:S(2)}, u32[]{:S(2)}) %all-to-all-start) | async-done | bytes 1179680 | tf_op jit(solution)/shard_map/all_to_all | solution.py:48
  40.4 9.7 %slice_reduce_fusion.2 = (bf16[128,1152]{1,0:T(8,128)(2,1)}, bf16[128,1152]{1,0:T(8,128)(2,1)S(1)}, bf16[128,1152]{1,0:T(8,128)(2,1)S(1)}, bf16[128,1152]{1,0:T(8,128)(2,1)S(1)}) fusion(bf16[4,1,128,1152]{3,0,1,2:T(4,128)(2,1)} %all-to-all-done), kind=kLoop, calls=%fused_computation.59 | loop fusion | bytes 2359296 | tf_op jit(solution)/shard_map/slice | solution.py:65
  50.1 2.7 %reshape_squeeze.6 = bf16[4,32,16,72]{3,2,1,0:T(8,128)(2,1)} reshape(bf16[128,1152]{1,0:T(8,128)(2,1)} %get-tuple-element.293) | data formatting | bytes 589824 | tf_op jit(solution)/shard_map/jvp()/reshape;squeeze | solution.py:14
  57.2 2.8 %fusion.50 = (f32[32,16,4]{2,1,0:T(8,128)S(1)}, f32[32,16,4,4]{2,3,1,0:T(4,128)S(1)}) fusion(bf16[4,32,16,72]{3,2,1,0:T(8,128)(2,1)} %reshape_squeeze.15, bf16[4,32,16,72]{3,2,1,0:T(8,128)(2,1)} %reshape_squeeze.14, pred[4]{0:T(512)(128)(4,1)S(1)} %iota_compare_fusion.1), kind=kOutput, calls=%fused_computation.92 | convolution fusion | flops 1202176 | bytes 630788 | tf_op jit(solution)/shard_map/jvp(qbhd,kbhd->bhqk)/dot_general | solution.py:15
  61.0 3.8 %convert_reduce_fusion = (f32[32,16,4]{2,1,0:T(8,128)}, pred[32,16,4,4]{2,3,1,0:T(4,128)(4,1)}, f32[32,16,4]{2,1,0:T(8,128)S(1)}, bf16[32,16,4,4]{2,3,1,0:T(4,128)(2,1)S(1)}) fusion(f32[32,16,4,4]{2,3,1,0:T(4,128)S(1)} %get-tuple-element.329, f32[32,16,4]{2,1,0:T(8,128)S(1)} %get-tuple-element.328, f32[32,16,4]{2,1,0:T(8,128)S(1)} %multiply_divide_fusion, ...), kind=kOutput, calls=%fused_computation.53 | convolution fusion | flops 1249280 | bytes 679936 | tf_op jit(solution)/shard_map/transpose(jvp(bhqk,kbhd->qbhd))/dot_general | solution.py:22
  64.9 2.7 %fusion.46 = (f32[32,16,4]{2,1,0:T(8,128)}, f32[32,16,4,4]{2,3,1,0:T(4,128)}, bf16[32,16,4,4]{2,3,1,0:T(4,128)(2,1)S(1)}) fusion(f32[32,16,4,4]{2,3,1,0:T(4,128)S(1)} %get-tuple-element.329, f32[32,16,4]{2,1,0:T(8,128)S(1)} %get-tuple-element.328, f32[32,16,4]{2,1,0:T(8,128)S(1)} %neg.9, f32[32,16,4]{2,1,0:T(8,128)S(1)} %fusion.45, ...), kind=kLoop, calls=%fused_computation.89 | loop fusion | flops 63488 | bytes 131072 | tf_op jit(solution)/shard_map/transpose(jvp())/reduce_sum | solution.py:19
  69.7 4.0 %all-to-all-start.3 = ((bf16[4,32,1152]{2,1,0:T(8,128)(2,1)}), bf16[4,32,1152]{2,1,0:T(8,128)(2,1)S(1)}, u32[]{:S(2)}, u32[]{:S(2)}) async-start(bf16[4,32,1152]{2,1,0:T(8,128)(2,1)} %convert_element_type.190), calls=%async_computation.3 | async-start | bytes 589824 | tf_op jit(solution)/shard_map/all_to_all | solution.py:68
  73.8 2.7 %convolution_convert_fusion.8 = bf16[16,128,72]{1,2,0:T(8,128)(2,1)} fusion(bf16[128,16,72]{0,2,1:T(8,128)(2,1)S(1)} %bitcast.87, f32[16,128]{1,0:T(8,128)S(1)} %copy-done.14, f32[16,128,128]{1,2,0:T(8,128)} %fusion.17), kind=kOutput, calls=%fused_computation.44 | convolution fusion | flops 38684800 | bytes 1646592 | tf_op jit(solution)/shard_map/bhqk,bkhd->bqhd/dot_general | solution.py:22
  76.5 2.7 %all-to-all-done.3 = bf16[4,32,1152]{2,1,0:T(8,128)(2,1)S(1)} async-done(((bf16[4,32,1152]{2,1,0:T(8,128)(2,1)}), bf16[4,32,1152]{2,1,0:T(8,128)(2,1)S(1)}, u32[]{:S(2)}, u32[]{:S(2)}) %all-to-all-start.3) | async-done | bytes 294944 | tf_op jit(solution)/shard_map/all_to_all | solution.py:68
  79.9 4.4 %all-to-all-start.2 = ((bf16[128,4,288]{0,2,1:T(8,128)(2,1)}), bf16[128,4,288]{0,2,1:T(8,128)(2,1)S(1)}, u32[]{:S(2)}, u32[]{:S(2)}) async-start(bf16[128,4,288]{0,2,1:T(8,128)(2,1)} %bitcast.88), calls=%async_computation.2 | async-start | bytes 589824 | tf_op jit(solution)/shard_map/all_to_all | solution.py:75
  86.6 3.1 %all-to-all-done.2 = bf16[128,4,288]{0,2,1:T(8,128)(2,1)S(1)} async-done(((bf16[128,4,288]{0,2,1:T(8,128)(2,1)}), bf16[128,4,288]{0,2,1:T(8,128)(2,1)S(1)}, u32[]{:S(2)}, u32[]{:S(2)}) %all-to-all-start.2) | async-done | bytes 294944 | tf_op jit(solution)/shard_map/all_to_all | solution.py:75
  89.7 5.0 %all-to-all-start.4 = ((bf16[128,4,288]{0,2,1:T(8,128)(2,1)}), bf16[128,4,288]{0,2,1:T(8,128)(2,1)}, u32[]{:S(2)}, u32[]{:S(2)}) async-start(bf16[128,4,288]{0,2,1:T(8,128)(2,1)} %copy.110), calls=%async_computation.4 | async-start | bytes 589824 | tf_op jit(solution)/shard_map/all_to_all | solution.py:76
  94.9 5.3 %all-to-all-done.4 = bf16[128,4,288]{0,2,1:T(8,128)(2,1)} async-done(((bf16[128,4,288]{0,2,1:T(8,128)(2,1)}), bf16[128,4,288]{0,2,1:T(8,128)(2,1)}, u32[]{:S(2)}, u32[]{:S(2)}) %all-to-all-start.4) | async-done | bytes 294944 | tf_op jit(solution)/shard_map/all_to_all | solution.py:76
  101.4 29.1 %while.16 = (s32[]{:T(128)}, f32[288,2,1152]{2,0,1:T(8,128)}, bf16[512,288]{1,0:T(8,128)(2,1)S(1)}, s32[]{:T(128)}, s32[]{:T(128)}, /*index=5*/bf16[512,1152]{1,...) while((s32[]{:T(128)}, f32[288,2,1152]{2,0,1:T(8,128)}, ...), condition=%wide.region_8.9_spmd.clone, body=%wide.region_7.8_spmd.clone.sunk | while | flops 174369792 | bytes 8787673 | solution.py:106
  111.5 3.6 %select_add_fusion.2 = f32[288,2,1152]{2,0,1:T(8,128)} fusion(f32[288,2,1152]{2,0,1:T(8,128)} %get-tuple-element.403, bf16[288,1,1152]{2,0,1:T(8,128)(2,1)S(1)} %fusion.67, bf16[288,1,1152]{2,0,1:T(8,128)(2,1)S(1)} %fusion.68, pred[]{:T(512)S(6)} %compare.19), kind=kLoop, calls=%fused_computation.clone.1 | loop fusion | flops 2654208 | bytes 6635521 | tf_op jit(solution)/shard_map/while/body/eval_jaxpr/add | solution.py:104
  119.2 3.6 %select_add_fusion.2 = f32[288,2,1152]{2,0,1:T(8,128)} fusion(f32[288,2,1152]{2,0,1:T(8,128)} %get-tuple-element.403, bf16[288,1,1152]{2,0,1:T(8,128)(2,1)S(1)} %fusion.67, bf16[288,1,1152]{2,0,1:T(8,128)(2,1)S(1)} %fusion.68, pred[]{:T(512)S(6)} %compare.19), kind=kLoop, calls=%fused_computation.clone.1 | loop fusion | flops 2654208 | bytes 6635521 | tf_op jit(solution)/shard_map/while/body/eval_jaxpr/add | solution.py:104
  126.9 3.6 %select_add_fusion.2 = f32[288,2,1152]{2,0,1:T(8,128)} fusion(f32[288,2,1152]{2,0,1:T(8,128)} %get-tuple-element.403, bf16[288,1,1152]{2,0,1:T(8,128)(2,1)S(1)} %fusion.67, bf16[288,1,1152]{2,0,1:T(8,128)(2,1)S(1)} %fusion.68, pred[]{:T(512)S(6)} %compare.19), kind=kLoop, calls=%fused_computation.clone.1 | loop fusion | flops 2654208 | bytes 6635521 | tf_op jit(solution)/shard_map/while/body/eval_jaxpr/add | solution.py:104
  130.5 3.6 %copy.113 = f32[288,2,1152]{0,2,1:T(8,128)} copy(f32[288,2,1152]{2,0,1:T(8,128)} %get-tuple-element.226) | data formatting | bytes 5308416 | tf_op jit(solution)/shard_map/while | solution.py:106
  136.1 2.6 %fusion.18 = bf16[4,32,16,72]{3,0,2,1:T(4,128)(2,1)S(1)} fusion(bf16[4,32,16,72]{3,2,1,0:T(8,128)(2,1)S(1)} %copy-done.7, f32[32,16,4,4]{2,3,1,0:T(4,128)} %get-tuple-element.316, pred[32,16,4,4]{2,3,1,0:T(4,128)(4,1)} %get-tuple-element.318, f32[32,16,4]{2,1,0:T(8,128)S(1)} %negate_divide_fusion, pred[4]{0:T(512)(128)(4,1)S(1)} %iota_compare_fusion.1), kind=kOutput, calls=%fused_computation.40 | convolution fusion | flops 1359872 | bytes 638980 | tf_op jit(solution)/shard_map/transpose(jvp(qbhd,kbhd->bhqk))/dot_general | solution.py:15
  139.4 2.6 %fusion.19 = bf16[4,32,16,72]{3,0,2,1:T(4,128)(2,1)S(1)} fusion(bf16[4,32,16,72]{3,2,1,0:T(8,128)(2,1)} %reshape_squeeze.14, f32[32,16,4,4]{2,3,1,0:T(4,128)} %get-tuple-element.316, pred[32,16,4,4]{2,3,1,0:T(4,128)(4,1)} %get-tuple-element.318, f32[32,16,4]{2,1,0:T(8,128)} %copy-done.11, pred[4]{0:T(512)(128)(4,1)S(1)} %iota_compare_fusion.1), kind=kOutput, calls=%fused_computation.41 | convolution fusion | flops 1359872 | bytes 638980 | tf_op jit(solution)/shard_map/transpose(jvp(qbhd,kbhd->bhqk))/dot_general | solution.py:15
  147.8 15.5 %all_to_all.62 = bf16[3,4,32,1152]{3,2,0,1:T(8,128)(2,1)S(1)} all-to-all(bf16[3,4,32,1152]{3,2,0,1:T(8,128)(2,1)S(1)} %copy.100), channel_id=1, replica_groups=mesh['dp'=8,'seq'=4] {'seq'}, dimensions={1} | all-to-all | bytes 1769472 | tf_op jit(solution)/shard_map/all_to_all | solution.py:69
  164.3 49.6 %reduce-scatter.2.cloned.1.call-done = f32[288,2,144]{0,2,1:T(8,128)} async-done(((f32[288,2,1152]{0,2,1:T(8,128)}), f32[288,2,144]{0,2,1:T(8,128)}) %reduce-scatter.2.cloned.1.call-update) | async-done | bytes 331792 | tf_op jit(solution)/shard_map/reduce_scatter | solution.py:107
  (95 shorter events, 56.1 us)
Async XLA Ops:
  7.2 4.3 %copy-start = (bf16[1152,1152]{1,0:T(8,128)(2,1)S(1)}, bf16[1152,1152]{1,0:T(8,128)(2,1)}, u32[]{:S(2)}) copy-start(bf16[1152,1152]{1,0:T(8,128)(2,1)} %param.14) | copy-start | bytes 7962628
  7.2 6.7 %copy-start.5 = (bf16[1,3,1,128,1152]{4,3,2,1,0:T(8,128)(2,1)S(1)}, bf16[1,3,1,128,1152]{4,3,2,1,0:T(8,128)(2,1)}, u32[]{:S(2)}) copy-start(bf16[1,3,1,128,1152]{4,3,2,1,0:T(8,128)(2,1)} %param.10) | copy-start | bytes 2654212
  7.2 94.2 %all-gather.3.cloned.1.call-start = ((), (), s32[]{:S(2)}) async-start(), calls=%async_computation.7 | async-start | bytes 1474560 | tf_op jit(solution)/shard_map/all_gather | solution.py:81
  16.9 23.5 %all-to-all-start = ((bf16[4,1,128,1152]{3,0,1,2:T(4,128)(2,1)}), bf16[4,1,128,1152]{3,0,1,2:T(4,128)(2,1)}, u32[]{:S(2)}, u32[]{:S(2)}) async-start(bf16[4,1,128,1152]{3,0,1,2:T(4,128)(2,1)} %pad_maximum_fusion), calls=%async_computation | async-start | bytes 2359296 | tf_op jit(solution)/shard_map/all_to_all | solution.py:48
  23.3 4.6 %copy-start.2 = (bf16[1,1,1,128,1152]{3,4,2,1,0:T(8,128)(2,1)S(1)}, bf16[1,1,1,128,1152]{3,4,2,1,0:T(8,128)(2,1)}, u32[]{:S(2)}) copy-start(bf16[1,1,1,128,1152]{3,4,2,1,0:T(8,128)(2,1)} %copy.103) | copy-start | bytes 884740
  24.1 3.7 %copy-start.3 = (bf16[1,1,1,128,1152]{3,4,2,1,0:T(8,128)(2,1)S(1)}, bf16[1,1,1,128,1152]{3,4,2,1,0:T(8,128)(2,1)}, u32[]{:S(2)}) copy-start(bf16[1,1,1,128,1152]{3,4,2,1,0:T(8,128)(2,1)} %copy.102) | copy-start | bytes 884740
  57.2 3.8 %copy-start.6 = (bf16[4,32,16,72]{3,2,1,0:T(8,128)(2,1)}, bf16[4,32,16,72]{3,2,1,0:T(8,128)(2,1)S(1)}, u32[]{:S(2)}) copy-start(bf16[4,32,16,72]{3,2,1,0:T(8,128)(2,1)S(1)} %reshape.200) | copy-start | bytes 884740
  57.2 3.8 %copy-start.8 = (bf16[4,32,16,72]{3,2,1,0:T(8,128)(2,1)S(1)}, bf16[4,32,16,72]{3,2,1,0:T(8,128)(2,1)}, u32[]{:S(2)}) copy-start(bf16[4,32,16,72]{3,2,1,0:T(8,128)(2,1)} %reshape_squeeze.6) | copy-start | bytes 884740
  67.6 0.9 copy-start.9
  67.6 6.2 %copy-start.10 = (bf16[1,1,1,128,1152]{3,4,2,1,0:T(8,128)(2,1)S(1)}, bf16[1,1,1,128,1152]{3,4,2,1,0:T(8,128)(2,1)}, u32[]{:S(2)}) copy-start(bf16[1,1,1,128,1152]{3,4,2,1,0:T(8,128)(2,1)} %copy.104) | copy-start | bytes 884740
  67.6 6.2 %copy-start.14 = (f32[16,128]{1,0:T(8,128)S(1)}, f32[16,128]{1,0:T(8,128)}, u32[]{:S(2)}) copy-start(f32[16,128]{1,0:T(8,128)} %fusion.51) | copy-start | bytes 24580
  69.7 9.4 %all-to-all-start.3 = ((bf16[4,32,1152]{2,1,0:T(8,128)(2,1)}), bf16[4,32,1152]{2,1,0:T(8,128)(2,1)S(1)}, u32[]{:S(2)}, u32[]{:S(2)}) async-start(bf16[4,32,1152]{2,1,0:T(8,128)(2,1)} %convert_element_type.190), calls=%async_computation.3 | async-start | bytes 589824 | tf_op jit(solution)/shard_map/all_to_all | solution.py:68
  76.5 24.9 %copy-start.12 = (f32[1,1152]{1,0:T(1,128)S(1)}, f32[1,1152]{1,0:T(1,128)}, u32[]{:S(2)}) copy-start(f32[1,1152]{1,0:T(1,128)} %param.13) | copy-start | bytes 13828
  76.5 24.9 %copy-start.13 = (f32[1,1152]{1,0:T(1,128)S(1)}, f32[1,1152]{1,0:T(1,128)}, u32[]{:S(2)}) copy-start(f32[1,1152]{1,0:T(1,128)} %param.12) | copy-start | bytes 13828
  79.2 0.7 copy-start.1
  79.9 9.8 %all-to-all-start.2 = ((bf16[128,4,288]{0,2,1:T(8,128)(2,1)}), bf16[128,4,288]{0,2,1:T(8,128)(2,1)S(1)}, u32[]{:S(2)}, u32[]{:S(2)}) async-start(bf16[128,4,288]{0,2,1:T(8,128)(2,1)} %bitcast.88), calls=%async_computation.2 | async-start | bytes 589824 | tf_op jit(solution)/shard_map/all_to_all | solution.py:75
  89.7 10.5 %all-to-all-start.4 = ((bf16[128,4,288]{0,2,1:T(8,128)(2,1)}), bf16[128,4,288]{0,2,1:T(8,128)(2,1)}, u32[]{:S(2)}, u32[]{:S(2)}) async-start(bf16[128,4,288]{0,2,1:T(8,128)(2,1)} %copy.110), calls=%async_computation.4 | async-start | bytes 589824 | tf_op jit(solution)/shard_map/all_to_all | solution.py:76
  94.7 119.1 %reduce-scatter.2.cloned.1.call-start = ((), (), s32[]{:S(2)}) async-start(), calls=%async_computation.6 | async-start | bytes 3981312 | tf_op jit(solution)/shard_map/reduce_scatter | solution.py:107
  134.2 0.9 copy-start.4
  134.2 2.0 copy-start.7
  136.1 2.7 %copy-start.11 = (f32[32,16,4]{2,1,0:T(8,128)}, f32[32,16,4]{2,1,0:T(8,128)S(1)}, u32[]{:S(2)}) copy-start(f32[32,16,4]{2,1,0:T(8,128)S(1)} %negate_divide_fusion) | copy-start | bytes 24580
Sparse Core Ops, SparseCore 0:
  9.6 23.0 all-gather.2
  134.3 79.5 reduce-scatter.1
where the time goes:
time: 225 us; the launch traced here: 223 us
  waiting for transfers between devices  72.5 us (32%)
  local copies, waits for them, and re-layouts  39.9 us (18%)
  matrix products  33.7 us (15%)
  other arithmetic  28 us (12%)
  starting transfers between devices  17.8 us (8%)
  blocking collectives  15.5 us (7%)
  between operations  14.9 us (7%)
    reduce_scatter x1, waiting for transfers between devices, body(): lax.psum_scatter(partial_sum, 'dp', scatter_dimension=2, tiled=True)  49.6 us
    all_to_all x1, blocking collectives, body(): lax.all_to_all(input_grads, 'seq', split_axis=1, concat_axis=2, tiled=True)  15.5 us
    add x4, other arithmetic, one_block(): return total + jnp.stack([part_first, part_second], axis=1)  12.6 us
    all_to_all x1, waiting for transfers between devices, body(): lax.all_to_all(stacked, 'seq', split_axis=2, concat_axis=1, tiled=True)  11.2 us
    slice x1, local copies, waits for them, and re-layouts, body(): exchanged[2]  9.68 us
    dot_general x4, matrix products, attend(): jnp.einsum(score_form, q_heads, k_heads, preferred_element_type=jnp.float32)  9.34 us
    dot_general x4, matrix products, attend(): jnp.einsum(mix_form, attention_weights, v_heads, preferred_element_type=j...  9.24 us
    dot_general x4, matrix products, one_block(): lax.dot_general(cols_first, error_first, (((0,), (0,)), ((), ())), prefer...  5.52 us
  transfers between devices with their start and end apart: 6, of which 5 were waited for; matrix products, arithmetic and copies ran while one was open for 29% of the time, Pallas kernels for 0%

commit v1 on v0

--- a/solution.py
+++ b/solution.py
@@ -1,10 +1,17 @@
+import functools
+
 import jax
 import jax.numpy as jnp
 from jax import lax
+from jax.experimental import pallas as pl
+from jax.experimental.pallas import tpu as pltpu
 from jax.sharding import PartitionSpec as P
 
 HEADS = 16
 HD = 72
+MESH = pl.DeviceIdType.MESH
+F32 = jnp.float32
+BF16 = jnp.bfloat16
 
 
 def attend(queries, key_block, value_block, key_keep, score_form, mix_form):
@@ -108,9 +115,330 @@
     return (grads_home[None], summed[:, 0], summed[:, 1])
 
 
+def kernel(
+    n, nb, counts, sgate, tgate, sqkv_hbm, tqkv_hbm, cot_hbm, proj_hbm,
+    g_out, sp_out, tp_out,
+    sqkv, tqkv, cot, proj, cot_t, q_t, v_t, o_t, so, so_r, tq, tq_r, tqf, gf,
+    err, err2, ot, do_t, part, xr, zs, zr, gs, gr,
+    loc_sem, cs, cr, fs, fr, ss, sr, ts, tr, us, ur, xss, xrs, zss, zrs,
+):
+    me = lax.axis_index("seq")
+    dp = lax.axis_index("dp")
+    pos, width = cot.shape
+    sl = width // n
+    rows = width // nb
+    ny, outer = n // 2, nb // 2
+    y, c = me // 2, me % 2
+    mate = y * 2 + 1 - c
+    oz, ox = dp // 2, dp % 2
+    scale = HD ** (-0.5)
+
+    loads = [
+        pltpu.make_async_copy(cot_hbm, cot, loc_sem.at[0]),
+        pltpu.make_async_copy(sqkv_hbm, sqkv, loc_sem.at[1]),
+        pltpu.make_async_copy(tqkv_hbm, tqkv, loc_sem.at[2]),
+        pltpu.make_async_copy(proj_hbm.at[me], proj, loc_sem.at[3]),
+    ]
+    for load in loads:
+        load.start()
+    barrier = pltpu.get_barrier_semaphore()
+    for j in range(1, n):
+        pl.semaphore_signal(barrier, inc=1, device_id=(dp, (me + j) % n), device_id_type=MESH)
+    pl.semaphore_signal(barrier, inc=1, device_id=(oz * 2 + 1 - ox, me), device_id_type=MESH)
+    for j in range(1, outer):
+        pl.semaphore_signal(
+            barrier, inc=1, device_id=((oz + j) % outer * 2 + ox, me), device_id_type=MESH
+        )
+
+    def remote(src, dst, s_sem, r_sem, to):
+        return pltpu.make_async_remote_copy(
+            src_ref=src, dst_ref=dst, send_sem=s_sem, recv_sem=r_sem, device_id=to,
+            device_id_type=MESH,
+        )
+
+    def turned(value):
+        return value.astype(F32).T
+
+    loads[0].wait()
+    cot_t[me] = turned(cot[...]).astype(BF16)
+    pl.semaphore_wait(barrier, (n - 1) + 1 + (outer - 1))
+
+    sent = []
+
+    def send(copy):
+        copy.start()
+        sent.append(copy)
+
+    def y_copy(j):
+        return remote(
+            cot_t.at[me], cot_t.at[me], cs.at[j - 1], cr.at[j - 1], (dp, (y + j) % ny * 2 + c)
+        )
+
+    def pass_copy(j, core):
+        slot = (y + ny - j) % ny * 2 + core
+        return remote(cot_t.at[slot], cot_t.at[slot], fs.at[j], fr.at[j], (dp, mate))
+
+    for j in range(1, ny):
+        send(y_copy(j))
+    send(pass_copy(0, c))
+
+    live_frames = counts[0, 0]
+    live_positions = counts[0, 1]
+
+    loads[1].wait()
+    q_t[...] = turned(sqkv[0])
+    v_t[...] = turned(sqkv[2])
+    key_keep = lax.broadcasted_iota(jnp.int32, (pos, pos), 0) < live_positions
+    for h in range(HEADS):
+        low = h * HD
+        w0 = low // 128 * 128
+        w1 = -(-(low + HD) // 128) * 128
+        row = lax.broadcasted_iota(jnp.int32, (w1 - w0, pos), 0)
+        inside = (row >= low - w0) & (row < low - w0 + HD)
+        q_win = jnp.where(inside, q_t[w0:w1, :], 0.0).astype(BF16)
+        scores = jnp.dot(sqkv[1, :, w0:w1], q_win, preferred_element_type=F32) * scale
+        scores = jnp.where(key_keep, scores, -1e30)
+        expo = jnp.exp(scores - jnp.max(scores, axis=0, keepdims=True))
+        weights = (expo / jnp.sum(expo, axis=0, keepdims=True)).astype(BF16)
+        o_t[low : low + HD, :] = jnp.dot(
+            v_t[low : low + HD, :].astype(BF16), weights, preferred_element_type=F32
+        )
+    for s in range(n):
+        so[s] = o_t[s * sl : (s + 1) * sl, :].astype(BF16)
+    so_r[me] = so[me]
+
+    def swap(src, dst, s_sem, r_sem, j):
+        to = (me + j) % n
+        return remote(src.at[to], dst.at[me], s_sem.at[j - 1], r_sem.at[j - 1], (dp, to))
+
+    def arrive(src, dst, s_sem, r_sem):
+        for j in range(1, n):
+            origin = (me + n - j) % n
+            remote(
+                src.at[origin], dst.at[origin], s_sem.at[j - 1], r_sem.at[j - 1], (dp, origin)
+            ).wait_recv()
+
+    for j in range(1, n):
+        send(swap(so, so_r, ss, sr, j))
+
+    loads[2].wait()
+    for m in range(3):
+        flat = turned(tqkv[m]).astype(BF16)
+        for s in range(n):
+            tq[s, m] = flat[s * sl : (s + 1) * sl, :]
+    tq_r[me] = tq[me]
+    for j in range(1, n):
+        send(swap(tq, tq_r, ts, tr, j))
+
+    def gate_rows(gate):
+        return jnp.broadcast_to(gate[...], (pos, width)).T
+
+    for j in range(1, ny):
+        slot = (y + ny - j) % ny * 2 + c
+        remote(
+            cot_t.at[slot], cot_t.at[slot], cs.at[j - 1], cr.at[j - 1], (dp, mate)
+        ).wait_recv()
+        send(pass_copy(j, c))
+    for j in range(ny):
+        pass_copy(j, 1 - c).wait_recv()
+
+    lane = lax.broadcasted_iota(jnp.int32, (1, pos), 1)
+    keep = [
+        ((lane < live_positions) & (f < live_frames)).astype(F32) for f in range(n)
+    ]
+
+    def errors(target, gate):
+        columns = gate_rows(gate)
+        for f in range(n):
+            target[:, f * pos : (f + 1) * pos] = (
+                keep[f] * cot_t[f].astype(F32) * columns
+            ).astype(BF16)
+
+    def product(p, source, outs):
+        for d in range(nb):
+            part[p, d] = lax.dot_general(
+                source[d * rows : (d + 1) * rows, :], outs, (((1,), (1,)), ((), ())),
+                preferred_element_type=F32,
+            ).astype(BF16)
+
+    def pair_copy(p, j):
+        z = (oz + j) % outer
+        return remote(
+            part.at[p, z * 2 + 1 - ox], xr.at[p, j], xss.at[p, j], xrs.at[p, j],
+            (oz * 2 + 1 - ox, me),
+        )
+
+    def line_copy(p, j):
+        z = (oz + j) % outer
+        return remote(
+            zs.at[p, j - 1], zr.at[p, j - 1], zss.at[p, j - 1], zrs.at[p, j - 1], (z * 2 + ox, me)
+        )
+
+    order = list(range(1, outer)) + [0]
+
+    def pair_start(p):
+        for j in order:
+            send(pair_copy(p, j))
+
+    def line_start(p):
+        for j in order:
+            z = (oz + j) % outer
+            pair_copy(p, j).wait_recv()
+            if j:
+                zs[p, j - 1] = (
+                    part[p, z * 2 + ox].astype(F32) + xr[p, j].astype(F32)
+                ).astype(BF16)
+                send(line_copy(p, j))
+
+    def line_end(p, out):
+        total = part[p, oz * 2 + ox].astype(F32) + xr[p, 0].astype(F32)
+        for j in range(1, outer):
+            line_copy(p, j).wait_recv()
+            total = total + zr[p, j - 1].astype(F32)
+        out[...] = total
+
+    errors(err, sgate)
+    arrive(so, so_r, ss, sr)
+    product(0, err, jnp.concatenate([so_r[f] for f in range(n)], axis=1))
+    pair_start(0)
+
+    errors(err2, tgate)
+    loads[3].wait()
+    do_t[...] = (
+        jnp.dot(proj[...], err2[...], preferred_element_type=F32).astype(BF16).astype(F32)
+    )
+    line_start(0)
+
+    arrive(tq, tq_r, ts, tr)
+    for f in range(n):
+        for m in range(3):
+            tqf[f, m] = tq_r[f, m].astype(F32)
+    kept = []
+    for h in range(sl // HD):
+        band = slice(h * HD, (h + 1) * HD)
+        ks = [tqf[g, 1, band, :] for g in range(n)]
+        vs = [tqf[g, 2, band, :] for g in range(n)]
+        for f in range(n):
+            q = tqf[f, 0, band, :]
+            row = [
+                jnp.where(g < live_frames, jnp.sum(q * ks[g], axis=0, keepdims=True) * scale, -1e30)
+                for g in range(n)
+            ]
+            top = functools.reduce(jnp.maximum, row)
+            expo = [jnp.exp(value - top) for value in row]
+            total = functools.reduce(jnp.add, expo)
+            soft = [value / total for value in expo]
+            rounded = [value.astype(BF16).astype(F32) for value in soft]
+            kept.append((soft, rounded))
+            ot[band, f * pos : (f + 1) * pos] = functools.reduce(
+                jnp.add, [rounded[g] * vs[g] for g in range(n)]
+            )
+    product(1, err2, ot[...].astype(BF16))
+    pair_start(1)
+
+    for h in range(sl // HD):
+        band = slice(h * HD, (h + 1) * HD)
+        slopes = []
+        for f in range(n):
+            soft, rounded = kept[h * n + f]
+            back = do_t[band, f * pos : (f + 1) * pos]
+            dw = [
+                jnp.sum(back * tqf[g, 2, band, :], axis=0, keepdims=True).astype(BF16).astype(F32)
+                for g in range(n)
+            ]
+            mean = functools.reduce(jnp.add, [soft[g] * dw[g] for g in range(n)])
+            slopes.append([soft[g] * (dw[g] - mean) * scale for g in range(n)])
+        for f in range(n):
+            gf[f, 0, band, :] = functools.reduce(
+                jnp.add, [slopes[f][g] * tqf[g, 1, band, :] for g in range(n)]
+            )
+            gf[f, 1, band, :] = functools.reduce(
+                jnp.add, [slopes[g][f] * tqf[g, 0, band, :] for g in range(n)]
+            )
+            gf[f, 2, band, :] = functools.reduce(
+                jnp.add,
+                [
+                    kept[h * n + g][1][f] * do_t[band, g * pos : (g + 1) * pos]
+                    for g in range(n)
+                ],
+            )
+    for f in range(n):
+        for m in range(3):
+            gs[f, m] = gf[f, m].astype(BF16)
+    gr[me] = gs[me]
+    for j in range(1, n):
+        send(swap(gs, gr, us, ur, j))
+
+    line_end(0, sp_out)
+    line_start(1)
+    arrive(gs, gr, us, ur)
+    for s in range(n):
+        for m in range(3):
+            g_out[m, s * sl : (s + 1) * sl, :] = gr[s, m]
+    line_end(1, tp_out)
+    for copy in sent:
+        copy.wait_send()
+
+
+def kernel_body(
+    n, nb, spatial_qkv, temporal_qkv, cotangent, spatial_gate, temporal_gate, temporal_proj, live_counts
+):
+    pos, width = cotangent.shape[2:]
+    sl, rows, outer, ny = width // n, width // nb, nb // 2, n // 2
+    vm, dma = pltpu.VMEM, pltpu.SemaphoreType.DMA
+    whole = pl.BlockSpec(memory_space=pltpu.VMEM)
+    left = pl.BlockSpec(memory_space=pl.ANY)
+    grads, first, second = pl.pallas_call(
+        functools.partial(kernel, n, nb),
+        out_shape=(
+            jax.ShapeDtypeStruct((3, width, pos), BF16),
+            jax.ShapeDtypeStruct((rows, sl), F32),
+            jax.ShapeDtypeStruct((rows, sl), F32),
+        ),
+        in_specs=[pl.BlockSpec(memory_space=pltpu.SMEM), whole, whole, left, left, left, left],
+        out_specs=(whole, whole, whole),
+        scratch_shapes=[
+            vm((3, pos, width), BF16), vm((3, pos, width), BF16), vm((pos, width), BF16),
+            vm((sl, width), BF16), vm((n, width, pos), BF16),
+            vm((width, pos), F32), vm((width, pos), F32), vm((width, pos), F32),
+            vm((n, sl, pos), BF16), vm((n, sl, pos), BF16),
+            vm((n, 3, sl, pos), BF16), vm((n, 3, sl, pos), BF16),
+            vm((n, 3, sl, pos), F32), vm((n, 3, sl, pos), F32),
+            vm((width, n * pos), BF16), vm((width, n * pos), BF16),
+            vm((sl, n * pos), F32), vm((sl, n * pos), F32),
+            vm((2, nb, rows, sl), BF16), vm((2, outer, rows, sl), BF16),
+            vm((2, outer - 1, rows, sl), BF16), vm((2, outer - 1, rows, sl), BF16),
+            vm((n, 3, sl, pos), BF16), vm((n, 3, sl, pos), BF16),
+            dma((4,)), dma((ny - 1,)), dma((ny - 1,)), dma((ny,)), dma((ny,)),
+            dma((n - 1,)), dma((n - 1,)), dma((n - 1,)), dma((n - 1,)), dma((n - 1,)), dma((n - 1,)),
+            dma((2, outer)), dma((2, outer)), dma((2, outer - 1)), dma((2, outer - 1)),
+        ],
+        compiler_params=pltpu.CompilerParams(
+            collective_id=0, has_side_effects=True, vmem_limit_bytes=56 * 1024 * 1024
+        ),
+    )(
+        live_counts, spatial_gate, temporal_gate,
+        spatial_qkv.reshape(3, pos, width), temporal_qkv.reshape(3, pos, width),
+        cotangent.reshape(pos, width), temporal_proj.reshape(n, sl, width),
+    )
+    grads = grads.transpose(0, 2, 1)[None, :, None]
+    return grads, first.T, second.T
+
+
 def solution(mesh):
+    n, nb = mesh.shape["seq"], mesh.shape["dp"]
+
+    def chosen(*args):
+        cot = args[2]
+        _, frames, pos, width = cot.shape
+        fits = frames == 1 and pos == 128 and width == HEADS * HD and n % 2 == 0 and nb % 2 == 0
+        fits = fits and n > 2 and nb > 2 and HEADS % n == 0
+        if fits and width // n % 16 == 0 and width // nb % 16 == 0:
+            return kernel_body(n, nb, *args)
+        return body(*args)
+
     return jax.shard_map(
-        body,
+        chosen,
         mesh=mesh,
         in_specs=(
             P("dp", None, "seq", None, None),

time: 225 us -> 54.9 us (0.24)
  waiting for transfers between devices: 72.5 us -> 0 us
  Pallas kernels: 0 us -> 47.9 us
  local copies, waits for them, and re-layouts: 39.9 us -> 5.49 us
  matrix products: 33.7 us -> 0 us
  other arithmetic: 28 us -> 0 us
  starting transfers between devices: 17.8 us -> 0 us
  blocking collectives: 15.5 us -> 0 us
  between operations: 14.9 us -> 0.64 us
    reduce_scatter x1 -> x0, waiting for transfers between devices: 49.6 us -> none  [body(): lax.psum_scatter(partial_sum, 'dp', scatter_dimension=2, tiled=True)]
    pallas_call x0 -> x1, Pallas kernels: none -> 47.9 us  [kernel_body(): pl.pallas_call(functools.partial(kernel, n, nb), out_shape=(jax.ShapeDtyp...]
    dot_general x17 -> x0, matrix products: 31.5 us -> none  [the longest x4 9.34 us: attend(): jnp.einsum(score_form, q_heads, k_heads, preferred_element_type=jnp.float32)]
    all_to_all x4 -> x0, waiting for transfers between devices: 22.2 us -> none  [the longest x1 11.2 us: body(): lax.all_to_all(stacked, 'seq', split_axis=2, concat_axis=1, tiled=True)]
    all_to_all x4 -> x0, starting transfers between devices: 17.7 us -> none  [the longest x1 5.03 us: body(): lax.all_to_all(flat_temporal, 'seq', split_axis=1, concat_axis=0, tiled=T...]
    all_to_all x1 -> x0, blocking collectives: 15.5 us -> none  [body(): lax.all_to_all(input_grads, 'seq', split_axis=1, concat_axis=2, tiled=True)]
    slice x6 -> x0, local copies, waits for them, and re-layouts: 15.1 us -> none  [the longest x1 9.68 us: body(): exchanged[2]]
    add x4 -> x0, other arithmetic: 12.6 us -> none  [one_block(): return total + jnp.stack([part_first, part_second], axis=1)]
  transfers between devices with their start and end apart: 6 -> 0, of which waited for: 5 -> 0; matrix products, arithmetic and copies ran while one was open for 29% -> 0% of each run, Pallas kernels for 0% -> 0%
where the time goes in v1:
time: 54.9 us; the launch traced here: 54 us
  Pallas kernels  47.9 us (87%)
  local copies, waits for them, and re-layouts  5.49 us (10%)
  between operations  0.64 us (1%)
    pallas_call x1, Pallas kernels, kernel_body(): pl.pallas_call(functools.partial(kernel, n, nb), out_shape=(jax.ShapeDtyp...  47.9 us
    unnamed x3, local copies, waits for them, and re-layouts  5.49 us

profile of v1, /device:TPU:1, one launch (start us, length us, event | category | flops | bytes accessed | tf_op | source)
XLA Modules:
  0.0 54.0 jit_solution(13312814255458187102)
XLA Ops:
  0.6 47.9 %shard_map.94 = (bf16[3,1152,128]{2,1,0:T(8,128)(2,1)}, f32[144,288]{1,0:T(8,128)}, f32[144,288]{1,0:T(8,128)}) custom-call(s32[1,2]{1,0:T(1,128)} %counts.1, f32[1,1152]{1,0:T(1,128)} %sgate.1, f32[1,1152]{1,0:T(1,128)} %tgate.1, bf16[3,128,1152]{2,1,0:T(8,128)(2,1)} %bitcast.11, bf16[3,128,1152]{2,1,0:T(8,128)(2,1)} %bitcast.12, ...), custom_call_target="tpu_custom_call" | custom-call | tf_op jit(solution)/shard_map/pallas_call | solution.py:391
  48.5 2.2 %copy.10 = bf16[1,3,1,128,1152]{4,3,2,1,0:T(8,128)(2,1)} copy(bf16[1,3,1,128,1152]{3,4,1,2,0:T(8,128)(2,1)} %bitcast.10) | data formatting | bytes 1769472
  50.8 1.6 %copy.13 = f32[288,144]{0,1:T(8,128)} copy(f32[288,144]{0,1:T(8,128)} %bitcast.15) | data formatting | bytes 331776
  52.4 1.6 %copy.14 = f32[288,144]{0,1:T(8,128)} copy(f32[288,144]{0,1:T(8,128)} %bitcast.14) | data formatting | bytes 331776

commit v2 on v1

--- a/solution.py
+++ b/solution.py
@@ -116,8 +116,8 @@
 
 
 def kernel(
-    n, nb, counts, sgate, tgate, sqkv_hbm, tqkv_hbm, cot_hbm, proj_hbm,
-    g_out, sp_out, tp_out,
+    n, nb, groups, counts, sgate, tgate, sqkv_hbm, tqkv_hbm, cot_hbm, proj_hbm,
+    g_out, sum_out,
     sqkv, tqkv, cot, proj, cot_t, q_t, v_t, o_t, so, so_r, tq, tq_r, tqf, gf,
     err, err2, ot, do_t, part, xr, zs, zr, gs, gr,
     loc_sem, cs, cr, fs, fr, ss, sr, ts, tr, us, ur, xss, xrs, zss, zrs,
@@ -127,6 +127,9 @@
     pos, width = cot.shape
     sl = width // n
     rows = width // nb
+    pieces = tq.shape[1]
+    half = sl // pieces
+    main = sl // 128 * 128
     ny, outer = n // 2, nb // 2
     y, c = me // 2, me % 2
     mate = y * 2 + 1 - c
@@ -204,31 +207,38 @@
             v_t[low : low + HD, :].astype(BF16), weights, preferred_element_type=F32
         )
     for s in range(n):
-        so[s] = o_t[s * sl : (s + 1) * sl, :].astype(BF16)
+        so[s, 0] = o_t[s * sl : (s + 1) * sl, :].astype(BF16)
     so_r[me] = so[me]
 
-    def swap(src, dst, s_sem, r_sem, j):
-        to = (me + j) % n
-        return remote(src.at[to], dst.at[me], s_sem.at[j - 1], r_sem.at[j - 1], (dp, to))
-
-    def arrive(src, dst, s_sem, r_sem):
+    def swap(src, dst, s_sem, r_sem, i=0):
+        for j in range(1, n):
+            to = (me + j) % n
+            send(
+                remote(
+                    src.at[to, i], dst.at[me, i], s_sem.at[i, j - 1], r_sem.at[i, j - 1], (dp, to)
+                )
+            )
+
+    def arrive(src, dst, s_sem, r_sem, i=0):
         for j in range(1, n):
             origin = (me + n - j) % n
             remote(
-                src.at[origin], dst.at[origin], s_sem.at[j - 1], r_sem.at[j - 1], (dp, origin)
+                src.at[origin, i], dst.at[origin, i], s_sem.at[i, j - 1], r_sem.at[i, j - 1],
+                (dp, origin),
             ).wait_recv()
 
-    for j in range(1, n):
-        send(swap(so, so_r, ss, sr, j))
+    swap(so, so_r, ss, sr)
 
     loads[2].wait()
     for m in range(3):
         flat = turned(tqkv[m]).astype(BF16)
         for s in range(n):
-            tq[s, m] = flat[s * sl : (s + 1) * sl, :]
+            for i in range(pieces):
+                low = s * sl + i * half
+                tq[s, i, m] = flat[low : low + half, :]
     tq_r[me] = tq[me]
-    for j in range(1, n):
-        send(swap(tq, tq_r, ts, tr, j))
+    for i in range(pieces):
+        swap(tq, tq_r, ts, tr, i)
 
     def gate_rows(gate):
         return jnp.broadcast_to(gate[...], (pos, width)).T
@@ -254,12 +264,44 @@
                 keep[f] * cot_t[f].astype(F32) * columns
             ).astype(BF16)
 
+    order = list(range(1, outer)) + [0]
+
+    def times(left, right):
+        return lax.dot_general(left, right, (((1,), (1,)), ((), ())), preferred_element_type=F32)
+
     def product(p, source, outs):
-        for d in range(nb):
-            part[p, d] = lax.dot_general(
-                source[d * rows : (d + 1) * rows, :], outs, (((1,), (1,)), ((), ())),
-                preferred_element_type=F32,
-            ).astype(BF16)
+        tail = sl - main
+        if tail:
+            short = rows // groups
+            edges = []
+            for k in range(groups):
+                blank = [
+                    jnp.zeros((size, outs.shape[1]), BF16)
+                    for size in (k * tail, 128 - (k + 1) * tail)
+                ]
+                parts = [blank[0], outs[main:, :], blank[1]]
+                edges.append(jnp.concatenate([v for v in parts if v.shape[0]], axis=0))
+        for x in (1 - ox, ox):
+            for j in order:
+                d = (oz + j) % outer * 2 + x
+                first = pl.multiple_of(d * rows, 16)
+                wide = times(source[pl.ds(first, rows), :], outs[:main, :]).astype(BF16)
+                for k in range(main // 128):
+                    part[p, d, k * rows : (k + 1) * rows, :] = wide[:, k * 128 : (k + 1) * 128]
+                if tail:
+                    edge = functools.reduce(
+                        jnp.add,
+                        [
+                            times(
+                                source[pl.ds(pl.multiple_of(first + k * short, 16), short), :],
+                                edges[k],
+                            )
+                            for k in range(groups)
+                        ],
+                    )
+                    part[p, d, main // 128 * rows :, :] = edge.astype(BF16)
+                if x is not ox:
+                    send(pair_copy(p, j))
 
     def pair_copy(p, j):
         z = (oz + j) % outer
@@ -273,12 +315,6 @@
         return remote(
             zs.at[p, j - 1], zr.at[p, j - 1], zss.at[p, j - 1], zrs.at[p, j - 1], (z * 2 + ox, me)
         )
-
-    order = list(range(1, outer)) + [0]
-
-    def pair_start(p):
-        for j in order:
-            send(pair_copy(p, j))
 
     def line_start(p):
         for j in order:
@@ -290,17 +326,16 @@
                 ).astype(BF16)
                 send(line_copy(p, j))
 
-    def line_end(p, out):
+    def line_end(p):
         total = part[p, oz * 2 + ox].astype(F32) + xr[p, 0].astype(F32)
         for j in range(1, outer):
             line_copy(p, j).wait_recv()
             total = total + zr[p, j - 1].astype(F32)
-        out[...] = total
+        sum_out[p] = total
 
     errors(err, sgate)
     arrive(so, so_r, ss, sr)
-    product(0, err, jnp.concatenate([so_r[f] for f in range(n)], axis=1))
-    pair_start(0)
+    product(0, err, jnp.concatenate([so_r[f, 0] for f in range(n)], axis=1))
 
     errors(err2, tgate)
     loads[3].wait()
@@ -309,75 +344,104 @@
     )
     line_start(0)
 
-    arrive(tq, tq_r, ts, tr)
-    for f in range(n):
-        for m in range(3):
-            tqf[f, m] = tq_r[f, m].astype(F32)
-    kept = []
-    for h in range(sl // HD):
-        band = slice(h * HD, (h + 1) * HD)
-        ks = [tqf[g, 1, band, :] for g in range(n)]
-        vs = [tqf[g, 2, band, :] for g in range(n)]
+    heads = half // HD
+
+    def forward(i):
+        kept = []
         for f in range(n):
-            q = tqf[f, 0, band, :]
-            row = [
-                jnp.where(g < live_frames, jnp.sum(q * ks[g], axis=0, keepdims=True) * scale, -1e30)
-                for g in range(n)
-            ]
-            top = functools.reduce(jnp.maximum, row)
-            expo = [jnp.exp(value - top) for value in row]
-            total = functools.reduce(jnp.add, expo)
-            soft = [value / total for value in expo]
-            rounded = [value.astype(BF16).astype(F32) for value in soft]
-            kept.append((soft, rounded))
-            ot[band, f * pos : (f + 1) * pos] = functools.reduce(
-                jnp.add, [rounded[g] * vs[g] for g in range(n)]
-            )
-    product(1, err2, ot[...].astype(BF16))
-    pair_start(1)
-
-    for h in range(sl // HD):
-        band = slice(h * HD, (h + 1) * HD)
-        slopes = []
+            for m in range(3):
+                tqf[f, i, m] = tq_r[f, i, m].astype(F32)
+        for h in range(heads):
+            band = slice(h * HD, (h + 1) * HD)
+            place = slice(i * half + h * HD, i * half + (h + 1) * HD)
+            ks = [tqf[g, i, 1, band, :] for g in range(n)]
+            vs = [tqf[g, i, 2, band, :] for g in range(n)]
+            for f in range(n):
+                q = tqf[f, i, 0, band, :]
+                row = [
+                    jnp.where(
+                        g < live_frames, jnp.sum(q * ks[g], axis=0, keepdims=True) * scale, -1e30
+                    )
+                    for g in range(n)
+                ]
+                top = functools.reduce(jnp.maximum, row)
+                expo = [jnp.exp(value - top) for value in row]
+                total = functools.reduce(jnp.add, expo)
+                soft = [value / total for value in expo]
+                rounded = [value.astype(BF16).astype(F32) for value in soft]
+                kept.append((soft, rounded))
+                ot[place, f * pos : (f + 1) * pos] = functools.reduce(
+                    jnp.add, [rounded[g] * vs[g] for g in range(n)]
+                )
+        return kept
+
+    def backward(i, kept):
+        for h in range(heads):
+            band = slice(h * HD, (h + 1) * HD)
+            place = slice(i * half + h * HD, i * half + (h + 1) * HD)
+            backs = [do_t[place, f * pos : (f + 1) * pos] for f in range(n)]
+            slopes = []
+            for f in range(n):
+                soft, _ = kept[h * n + f]
+                dw = [
+                    jnp.sum(backs[f] * tqf[g, i, 2, band, :], axis=0, keepdims=True)
+                    .astype(BF16)
+                    .astype(F32)
+                    for g in range(n)
+                ]
+                mean = functools.reduce(jnp.add, [soft[g] * dw[g] for g in range(n)])
+                slopes.append([soft[g] * (dw[g] - mean) * scale for g in range(n)])
+            for f in range(n):
+                gf[f, i, 0, band, :] = functools.reduce(
+                    jnp.add, [slopes[f][g] * tqf[g, i, 1, band, :] for g in range(n)]
+                )
+                gf[f, i, 1, band, :] = functools.reduce(
+                    jnp.add, [slopes[g][f] * tqf[g, i, 0, band, :] for g in range(n)]
+                )
+                gf[f, i, 2, band, :] = functools.reduce(
+                    jnp.add, [kept[h * n + g][1][f] * backs[g] for g in range(n)]
+                )
         for f in range(n):
-            soft, rounded = kept[h * n + f]
-            back = do_t[band, f * pos : (f + 1) * pos]
-            dw = [
-                jnp.sum(back * tqf[g, 2, band, :], axis=0, keepdims=True).astype(BF16).astype(F32)
-                for g in range(n)
-            ]
-            mean = functools.reduce(jnp.add, [soft[g] * dw[g] for g in range(n)])
-            slopes.append([soft[g] * (dw[g] - mean) * scale for g in range(n)])
-        for f in range(n):
-            gf[f, 0, band, :] = functools.reduce(
-                jnp.add, [slopes[f][g] * tqf[g, 1, band, :] for g in range(n)]
-            )
-            gf[f, 1, band, :] = functools.reduce(
-                jnp.add, [slopes[g][f] * tqf[g, 0, band, :] for g in range(n)]
-            )
-            gf[f, 2, band, :] = functools.reduce(
-                jnp.add,
-                [
-                    kept[h * n + g][1][f] * do_t[band, g * pos : (g + 1) * pos]
-                    for g in range(n)
-                ],
-            )
-    for f in range(n):
-        for m in range(3):
-            gs[f, m] = gf[f, m].astype(BF16)
+            for m in range(3):
+                gs[f, i, m] = gf[f, i, m].astype(BF16)
+        swap(gs, gr, us, ur, i)
+
+    for i in range(pieces):
+        arrive(tq, tq_r, ts, tr, i)
+        kept = forward(i)
+        if i == pieces - 1:
+            product(1, err2, ot[...].astype(BF16))
+        backward(i, kept)
     gr[me] = gs[me]
-    for j in range(1, n):
-        send(swap(gs, gr, us, ur, j))
-
-    line_end(0, sp_out)
+
+    line_end(0)
     line_start(1)
-    arrive(gs, gr, us, ur)
-    for s in range(n):
-        for m in range(3):
-            g_out[m, s * sl : (s + 1) * sl, :] = gr[s, m]
-    line_end(1, tp_out)
+    for i in range(pieces):
+        arrive(gs, gr, us, ur, i)
+        for s in range(n):
+            for m in range(3):
+                low = s * sl + i * half
+                g_out[m, low : low + half, :] = gr[s, i, m]
+    line_end(1)
     for copy in sent:
         copy.wait_send()
+
+
+def finish(nb, groups, grads, sums, g_out, sp_out, tp_out):
+    g_out[0] = grads[0].astype(F32).T.astype(BF16)
+    rows, sl = sp_out.shape
+    main, short = sl // 128 * 128, rows // groups
+    tail = sl - main
+
+    @pl.when(pl.program_id(0) == 0)
+    def _():
+        for p, out in enumerate((sp_out, tp_out)):
+            for k in range(main // 128):
+                out[:, k * 128 : (k + 1) * 128] = sums[p, k * rows : (k + 1) * rows, :]
+            if tail:
+                edge = sums[p, main // 128 * rows :, :]
+                for k in range(groups):
+                    out[k * short : (k + 1) * short, main:] = edge[:, k * tail : (k + 1) * tail]
 
 
 def kernel_body(
@@ -388,29 +452,35 @@
     vm, dma = pltpu.VMEM, pltpu.SemaphoreType.DMA
     whole = pl.BlockSpec(memory_space=pltpu.VMEM)
     left = pl.BlockSpec(memory_space=pl.ANY)
-    grads, first, second = pl.pallas_call(
-        functools.partial(kernel, n, nb),
+    pieces = 2 if sl // HD % 2 == 0 and sl // 2 % 16 == 0 else 1
+    half, tail = sl // pieces, sl % 128
+    groups = 1
+    if tail:
+        groups = max(g for g in range(1, 128 // tail + 1) if rows % (16 * g) == 0)
+    packed = sl // 128 * rows + (rows // groups if tail else 0)
+    grads, sums = pl.pallas_call(
+        functools.partial(kernel, n, nb, groups),
         out_shape=(
             jax.ShapeDtypeStruct((3, width, pos), BF16),
-            jax.ShapeDtypeStruct((rows, sl), F32),
-            jax.ShapeDtypeStruct((rows, sl), F32),
+            jax.ShapeDtypeStruct((2, packed, 128), F32),
         ),
         in_specs=[pl.BlockSpec(memory_space=pltpu.SMEM), whole, whole, left, left, left, left],
-        out_specs=(whole, whole, whole),
+        out_specs=(whole, whole),
         scratch_shapes=[
             vm((3, pos, width), BF16), vm((3, pos, width), BF16), vm((pos, width), BF16),
             vm((sl, width), BF16), vm((n, width, pos), BF16),
             vm((width, pos), F32), vm((width, pos), F32), vm((width, pos), F32),
-            vm((n, sl, pos), BF16), vm((n, sl, pos), BF16),
-            vm((n, 3, sl, pos), BF16), vm((n, 3, sl, pos), BF16),
-            vm((n, 3, sl, pos), F32), vm((n, 3, sl, pos), F32),
+            vm((n, 1, sl, pos), BF16), vm((n, 1, sl, pos), BF16),
+            vm((n, pieces, 3, half, pos), BF16), vm((n, pieces, 3, half, pos), BF16),
+            vm((n, pieces, 3, half, pos), F32), vm((n, pieces, 3, half, pos), F32),
             vm((width, n * pos), BF16), vm((width, n * pos), BF16),
             vm((sl, n * pos), F32), vm((sl, n * pos), F32),
-            vm((2, nb, rows, sl), BF16), vm((2, outer, rows, sl), BF16),
-            vm((2, outer - 1, rows, sl), BF16), vm((2, outer - 1, rows, sl), BF16),
-            vm((n, 3, sl, pos), BF16), vm((n, 3, sl, pos), BF16),
+            vm((2, nb, packed, 128), BF16), vm((2, outer, packed, 128), BF16),
+            vm((2, outer - 1, packed, 128), BF16), vm((2, outer - 1, packed, 128), BF16),
+            vm((n, pieces, 3, half, pos), BF16), vm((n, pieces, 3, half, pos), BF16),
             dma((4,)), dma((ny - 1,)), dma((ny - 1,)), dma((ny,)), dma((ny,)),
-            dma((n - 1,)), dma((n - 1,)), dma((n - 1,)), dma((n - 1,)), dma((n - 1,)), dma((n - 1,)),
+            dma((1, n - 1)), dma((1, n - 1)), dma((pieces, n - 1)), dma((pieces, n - 1)),
+            dma((pieces, n - 1)), dma((pieces, n - 1)),
             dma((2, outer)), dma((2, outer)), dma((2, outer - 1)), dma((2, outer - 1)),
         ],
         compiler_params=pltpu.CompilerParams(
@@ -421,8 +491,26 @@
         spatial_qkv.reshape(3, pos, width), temporal_qkv.reshape(3, pos, width),
         cotangent.reshape(pos, width), temporal_proj.reshape(n, sl, width),
     )
-    grads = grads.transpose(0, 2, 1)[None, :, None]
-    return grads, first.T, second.T
+    fixed = lambda i: (0, 0)
+    grads, first, second = pl.pallas_call(
+        functools.partial(finish, nb, groups),
+        grid=(3,),
+        out_shape=(
+            jax.ShapeDtypeStruct((3, pos, width), BF16),
+            jax.ShapeDtypeStruct((rows, sl), F32),
+            jax.ShapeDtypeStruct((rows, sl), F32),
+        ),
+        in_specs=[
+            pl.BlockSpec((1, width, pos), lambda i: (i, 0, 0)),
+            pl.BlockSpec((2, packed, 128), lambda i: (0, 0, 0)),
+        ],
+        out_specs=(
+            pl.BlockSpec((1, pos, width), lambda i: (i, 0, 0)),
+            pl.BlockSpec((rows, sl), fixed),
+            pl.BlockSpec((rows, sl), fixed),
+        ),
+    )(grads, sums)
+    return grads[None, :, None], first.T, second.T
 
 
 def solution(mesh):

time: 54.9 us -> 46.7 us (0.85)
  local copies, waits for them, and re-layouts: 5.49 us -> 0 us
  Pallas kernels: 47.9 us -> 45.3 us
    unnamed x3 -> x0, local copies, waits for them, and re-layouts: 5.49 us -> none
    pallas_call x1 -> x2, Pallas kernels: 47.9 us -> 45.3 us  [the longest x1 41.8 us: kernel_body(): pl.pallas_call(functools.partial(kernel, n, nb, groups), out_shape=(jax.S...]
where the time goes in v2:
time: 46.7 us; the launch traced here: 45.9 us
  Pallas kernels  45.3 us (97%)
  between operations  0.64 us (1%)
    pallas_call x1, Pallas kernels, kernel_body(): pl.pallas_call(functools.partial(kernel, n, nb, groups), out_shape=(jax.S...  41.8 us
    pallas_call x1, Pallas kernels, kernel_body(): pl.pallas_call(functools.partial(finish, nb, groups), grid=(3,), out_shap...  3.42 us

profile of v2, /device:TPU:1, one launch (start us, length us, event | category | flops | bytes accessed | tf_op | source)
XLA Modules:
  0.0 45.9 jit_solution(16564297253301800423)
XLA Ops:
  0.6 41.8 %shard_map.94 = (bf16[3,1152,128]{2,1,0:T(8,128)(2,1)}, f32[2,336,128]{2,1,0:T(8,128)}) custom-call(s32[1,2]{1,0:T(1,128)} %counts.1, f32[1,1152]{1,0:T(1,128)} %sgate.1, f32[1,1152]{1,0:T(1,128)} %tgate.1, bf16[3,128,1152]{2,1,0:T(8,128)(2,1)} %bitcast.10, bf16[3,128,1152]{2,1,0:T(8,128)(2,1)} %bitcast.11, bf16[128,1152]{1,0:T(8,128)(2,1)} %bitcast.12, ...), custom_call_target="tpu_custom_call" | custom-call | tf_op jit(solution)/shard_map/pallas_call | solution.py:461
  42.5 3.4 %shard_map.95 = (bf16[3,128,1152]{2,1,0:T(8,128)(2,1)}, f32[144,288]{1,0:T(8,128)}, f32[144,288]{1,0:T(8,128)}) custom-call(bf16[3,1152,128]{2,1,0:T(8,128)(2,1)} %get-tuple-element.8.grads, f32[2,336,128]{2,1,0:T(8,128)} %get-tuple-element.9.sums), custom_call_target="tpu_custom_call" | custom-call | tf_op jit(solution)/shard_map/pallas_call | solution.py:495

commit v3 on v2

--- a/solution.py
+++ b/solution.py
@@ -116,7 +116,7 @@
 
 
 def kernel(
-    n, nb, groups, counts, sgate, tgate, sqkv_hbm, tqkv_hbm, cot_hbm, proj_hbm,
+    n, nb, units, counts, sgate, tgate, sqkv_hbm, tqkv_hbm, cot_hbm, proj_hbm,
     g_out, sum_out,
     sqkv, tqkv, cot, proj, cot_t, q_t, v_t, o_t, so, so_r, tq, tq_r, tqf, gf,
     err, err2, ot, do_t, part, xr, zs, zr, gs, gr,
@@ -129,7 +129,6 @@
     rows = width // nb
     pieces = tq.shape[1]
     half = sl // pieces
-    main = sl // 128 * 128
     ny, outer = n // 2, nb // 2
     y, c = me // 2, me % 2
     mate = y * 2 + 1 - c
@@ -270,7 +269,7 @@
         return lax.dot_general(left, right, (((1,), (1,)), ((), ())), preferred_element_type=F32)
 
     def product(p, source, outs):
-        tail = sl - main
+        main, tail, groups, _ = units[p]
         if tail:
             short = rows // groups
             edges = []
@@ -299,21 +298,22 @@
                             for k in range(groups)
                         ],
                     )
-                    part[p, d, main // 128 * rows :, :] = edge.astype(BF16)
+                    part[p, d, main // 128 * rows : units[p][3], :] = edge.astype(BF16)
                 if x is not ox:
                     send(pair_copy(p, j))
 
     def pair_copy(p, j):
         z = (oz + j) % outer
         return remote(
-            part.at[p, z * 2 + 1 - ox], xr.at[p, j], xss.at[p, j], xrs.at[p, j],
+            part.at[p, z * 2 + 1 - ox, : units[p][3]], xr.at[p, j, : units[p][3]], xss.at[p, j], xrs.at[p, j],
             (oz * 2 + 1 - ox, me),
         )
 
     def line_copy(p, j):
         z = (oz + j) % outer
         return remote(
-            zs.at[p, j - 1], zr.at[p, j - 1], zss.at[p, j - 1], zrs.at[p, j - 1], (z * 2 + ox, me)
+            zs.at[p, j - 1, : units[p][3]], zr.at[p, j - 1, : units[p][3]],
+            zss.at[p, j - 1], zrs.at[p, j - 1], (z * 2 + ox, me)
         )
 
     def line_start(p):
@@ -321,17 +321,19 @@
             z = (oz + j) % outer
             pair_copy(p, j).wait_recv()
             if j:
-                zs[p, j - 1] = (
-                    part[p, z * 2 + ox].astype(F32) + xr[p, j].astype(F32)
+                size = units[p][3]
+                zs[p, j - 1, :size, :] = (
+                    part[p, z * 2 + ox, :size, :].astype(F32) + xr[p, j, :size, :].astype(F32)
                 ).astype(BF16)
                 send(line_copy(p, j))
 
     def line_end(p):
-        total = part[p, oz * 2 + ox].astype(F32) + xr[p, 0].astype(F32)
+        size = units[p][3]
+        total = part[p, oz * 2 + ox, :size, :].astype(F32) + xr[p, 0, :size, :].astype(F32)
         for j in range(1, outer):
             line_copy(p, j).wait_recv()
-            total = total + zr[p, j - 1].astype(F32)
-        sum_out[p] = total
+            total = total + zr[p, j - 1, :size, :].astype(F32)
+        sum_out[p, :size, :] = total
 
     errors(err, sgate)
     arrive(so, so_r, ss, sr)
@@ -342,8 +344,6 @@
     do_t[...] = (
         jnp.dot(proj[...], err2[...], preferred_element_type=F32).astype(BF16).astype(F32)
     )
-    line_start(0)
-
     heads = half // HD
 
     def forward(i):
@@ -409,39 +409,58 @@
     for i in range(pieces):
         arrive(tq, tq_r, ts, tr, i)
         kept = forward(i)
-        if i == pieces - 1:
-            product(1, err2, ot[...].astype(BF16))
+        product(1 + i, err2, ot[i * half : (i + 1) * half, :].astype(BF16))
         backward(i, kept)
+        if i == 0:
+            line_start(0)
     gr[me] = gs[me]
 
     line_end(0)
-    line_start(1)
+    for i in range(pieces):
+        line_start(1 + i)
     for i in range(pieces):
         arrive(gs, gr, us, ur, i)
+    for m in range(3):
         for s in range(n):
-            for m in range(3):
+            for i in range(pieces):
                 low = s * sl + i * half
-                g_out[m, low : low + half, :] = gr[s, i, m]
-    line_end(1)
+                q_t[low : low + half, :] = gr[s, i, m].astype(F32)
+        g_out[m] = q_t[...].T.astype(BF16)
+    for i in range(pieces):
+        line_end(1 + i)
     for copy in sent:
         copy.wait_send()
 
 
-def finish(nb, groups, grads, sums, g_out, sp_out, tp_out):
-    g_out[0] = grads[0].astype(F32).T.astype(BF16)
-    rows, sl = sp_out.shape
-    main, short = sl // 128 * 128, rows // groups
-    tail = sl - main
+def finish(units, grads, sums, g_out, sp_out, tp_out):
+    g_out[...] = grads[...]
+    rows = sp_out.shape[0]
 
     @pl.when(pl.program_id(0) == 0)
     def _():
-        for p, out in enumerate((sp_out, tp_out)):
+        left = 0
+        for p, (main, tail, groups, size) in enumerate(units):
+            out = tp_out if p else sp_out
             for k in range(main // 128):
-                out[:, k * 128 : (k + 1) * 128] = sums[p, k * rows : (k + 1) * rows, :]
+                low = left + k * 128
+                out[:, low : low + 128] = sums[p, k * rows : (k + 1) * rows, :]
             if tail:
-                edge = sums[p, main // 128 * rows :, :]
+                short = rows // groups
+                edge = sums[p, main // 128 * rows : size, :]
+                low = left + main
                 for k in range(groups):
-                    out[k * short : (k + 1) * short, main:] = edge[:, k * tail : (k + 1) * tail]
+                    out[k * short : (k + 1) * short, low : low + tail] = edge[
+                        :, k * tail : (k + 1) * tail
+                    ]
+            left = left + main + tail if p else 0
+
+
+def unit_of(columns, rows):
+    main, tail = columns // 128 * 128, columns % 128
+    groups = 1
+    if tail:
+        groups = max(g for g in range(1, 128 // tail + 1) if rows % (16 * g) == 0)
+    return main, tail, groups, main // 128 * rows + (rows // groups if tail else 0)
 
 
 def kernel_body(
@@ -453,16 +472,14 @@
     whole = pl.BlockSpec(memory_space=pltpu.VMEM)
     left = pl.BlockSpec(memory_space=pl.ANY)
     pieces = 2 if sl // HD % 2 == 0 and sl // 2 % 16 == 0 else 1
-    half, tail = sl // pieces, sl % 128
-    groups = 1
-    if tail:
-        groups = max(g for g in range(1, 128 // tail + 1) if rows % (16 * g) == 0)
-    packed = sl // 128 * rows + (rows // groups if tail else 0)
+    half = sl // pieces
+    units = [unit_of(sl, rows)] + [unit_of(half, rows)] * pieces
+    count, packed = len(units), max(unit[3] for unit in units)
     grads, sums = pl.pallas_call(
-        functools.partial(kernel, n, nb, groups),
+        functools.partial(kernel, n, nb, units),
         out_shape=(
-            jax.ShapeDtypeStruct((3, width, pos), BF16),
-            jax.ShapeDtypeStruct((2, packed, 128), F32),
+            jax.ShapeDtypeStruct((3, pos, width), BF16),
+            jax.ShapeDtypeStruct((count, packed, 128), F32),
         ),
         in_specs=[pl.BlockSpec(memory_space=pltpu.SMEM), whole, whole, left, left, left, left],
         out_specs=(whole, whole),
@@ -475,13 +492,13 @@
             vm((n, pieces, 3, half, pos), F32), vm((n, pieces, 3, half, pos), F32),
             vm((width, n * pos), BF16), vm((width, n * pos), BF16),
             vm((sl, n * pos), F32), vm((sl, n * pos), F32),
-            vm((2, nb, packed, 128), BF16), vm((2, outer, packed, 128), BF16),
-            vm((2, outer - 1, packed, 128), BF16), vm((2, outer - 1, packed, 128), BF16),
+            vm((count, nb, packed, 128), BF16), vm((count, outer, packed, 128), BF16),
+            vm((count, outer - 1, packed, 128), BF16), vm((count, outer - 1, packed, 128), BF16),
             vm((n, pieces, 3, half, pos), BF16), vm((n, pieces, 3, half, pos), BF16),
             dma((4,)), dma((ny - 1,)), dma((ny - 1,)), dma((ny,)), dma((ny,)),
             dma((1, n - 1)), dma((1, n - 1)), dma((pieces, n - 1)), dma((pieces, n - 1)),
             dma((pieces, n - 1)), dma((pieces, n - 1)),
-            dma((2, outer)), dma((2, outer)), dma((2, outer - 1)), dma((2, outer - 1)),
+            dma((count, outer)), dma((count, outer)), dma((count, outer - 1)), dma((count, outer - 1)),
         ],
         compiler_params=pltpu.CompilerParams(
             collective_id=0, has_side_effects=True, vmem_limit_bytes=56 * 1024 * 1024
@@ -493,7 +510,7 @@
     )
     fixed = lambda i: (0, 0)
     grads, first, second = pl.pallas_call(
-        functools.partial(finish, nb, groups),
+        functools.partial(finish, units),
         grid=(3,),
         out_shape=(
             jax.ShapeDtypeStruct((3, pos, width), BF16),
@@ -501,8 +518,8 @@
             jax.ShapeDtypeStruct((rows, sl), F32),
         ),
         in_specs=[
-            pl.BlockSpec((1, width, pos), lambda i: (i, 0, 0)),
-            pl.BlockSpec((2, packed, 128), lambda i: (0, 0, 0)),
+            pl.BlockSpec((1, pos, width), lambda i: (i, 0, 0)),
+            pl.BlockSpec((count, packed, 128), lambda i: (0, 0, 0)),
         ],
         out_specs=(
             pl.BlockSpec((1, pos, width), lambda i: (i, 0, 0)),

time: 46.7 us -> 45.8 us (0.981); the launches traced: 45.9 us -> 45.6 us
  no operation moved by 1% of the time
where the time goes in v3:
time: 45.8 us; the launch traced here: 45.6 us
  Pallas kernels  44.9 us (98%)
  between operations  0.64 us (1%)
    pallas_call x1, Pallas kernels, kernel_body(): pl.pallas_call(functools.partial(kernel, n, nb, units), out_shape=(jax.Sh...  41.6 us
    pallas_call x1, Pallas kernels, kernel_body(): pl.pallas_call(functools.partial(finish, units), grid=(3,), out_shape=(ja...  3.36 us

profile of v3, /device:TPU:1, one launch (start us, length us, event | category | flops | bytes accessed | tf_op | source)
XLA Modules:
  0.0 45.6 jit_solution(4668891679910821941)
XLA Ops:
  0.6 41.6 %shard_map.94 = (bf16[3,128,1152]{2,1,0:T(8,128)(2,1)}, f32[3,336,128]{2,1,0:T(8,128)}) custom-call(s32[1,2]{1,0:T(1,128)} %counts.1, f32[1,1152]{1,0:T(1,128)} %sgate.1, f32[1,1152]{1,0:T(1,128)} %tgate.1, bf16[3,128,1152]{2,1,0:T(8,128)(2,1)} %bitcast.10, bf16[3,128,1152]{2,1,0:T(8,128)(2,1)} %bitcast.11, bf16[128,1152]{1,0:T(8,128)(2,1)} %bitcast.12, ...), custom_call_target="tpu_custom_call" | custom-call | tf_op jit(solution)/shard_map/pallas_call | solution.py:478
  42.2 3.4 %shard_map.95 = (bf16[3,128,1152]{2,1,0:T(8,128)(2,1)}, f32[144,288]{1,0:T(8,128)}, f32[144,288]{1,0:T(8,128)}) custom-call(bf16[3,128,1152]{2,1,0:T(8,128)(2,1)} %get-tuple-element.8.grads, f32[3,336,128]{2,1,0:T(8,128)} %get-tuple-element.9.sums), custom_call_target="tpu_custom_call" | custom-call | tf_op jit(solution)/shard_map/pallas_call | solution.py:512

commit v4 on v3

--- a/solution.py
+++ b/solution.py
@@ -511,18 +511,18 @@
     fixed = lambda i: (0, 0)
     grads, first, second = pl.pallas_call(
         functools.partial(finish, units),
-        grid=(3,),
+        grid=(1,),
         out_shape=(
             jax.ShapeDtypeStruct((3, pos, width), BF16),
             jax.ShapeDtypeStruct((rows, sl), F32),
             jax.ShapeDtypeStruct((rows, sl), F32),
         ),
         in_specs=[
-            pl.BlockSpec((1, pos, width), lambda i: (i, 0, 0)),
+            pl.BlockSpec((3, pos, width), lambda i: (0, 0, 0)),
             pl.BlockSpec((count, packed, 128), lambda i: (0, 0, 0)),
         ],
         out_specs=(
-            pl.BlockSpec((1, pos, width), lambda i: (i, 0, 0)),
+            pl.BlockSpec((3, pos, width), lambda i: (0, 0, 0)),
             pl.BlockSpec((rows, sl), fixed),
             pl.BlockSpec((rows, sl), fixed),
         ),

time: 45.8 us -> 44.9 us (0.980)
  Pallas kernels: 44.9 us -> 44 us
    pallas_call x1, Pallas kernels: 3.36 us -> 2.43 us  [kernel_body(): pl.pallas_call(functools.partial(finish, units), grid=(1,), out_shape=(ja...]
where the time goes in v4:
time: 44.9 us; the launch traced here: 44.7 us
  Pallas kernels  44 us (98%)
  between operations  0.64 us (1%)
    pallas_call x1, Pallas kernels, kernel_body(): pl.pallas_call(functools.partial(kernel, n, nb, units), out_shape=(jax.Sh...  41.6 us
    pallas_call x1, Pallas kernels, kernel_body(): pl.pallas_call(functools.partial(finish, units), grid=(1,), out_shape=(ja...  2.43 us

profile of v4, /device:TPU:1, one launch (start us, length us, event | category | flops | bytes accessed | tf_op | source)
XLA Modules:
  0.0 44.7 jit_solution(17971982695222461008)
XLA Ops:
  0.6 41.6 %shard_map.94 = (bf16[3,128,1152]{2,1,0:T(8,128)(2,1)}, f32[3,336,128]{2,1,0:T(8,128)}) custom-call(s32[1,2]{1,0:T(1,128)} %counts.1, f32[1,1152]{1,0:T(1,128)} %sgate.1, f32[1,1152]{1,0:T(1,128)} %tgate.1, bf16[3,128,1152]{2,1,0:T(8,128)(2,1)} %bitcast.10, bf16[3,128,1152]{2,1,0:T(8,128)(2,1)} %bitcast.11, bf16[128,1152]{1,0:T(8,128)(2,1)} %bitcast.12, ...), custom_call_target="tpu_custom_call" | custom-call | tf_op jit(solution)/shard_map/pallas_call | solution.py:478
  42.2 2.4 %shard_map.95 = (bf16[3,128,1152]{2,1,0:T(8,128)(2,1)}, f32[144,288]{1,0:T(8,128)}, f32[144,288]{1,0:T(8,128)}) custom-call(bf16[3,128,1152]{2,1,0:T(8,128)(2,1)} %get-tuple-element.8.grads, f32[3,336,128]{2,1,0:T(8,128)} %get-tuple-element.9.sums), custom_call_target="tpu_custom_call" | custom-call | tf_op jit(solution)/shard_map/pallas_call | solution.py:512
